TPU v7x, 32 devices: a whole 2x2x4 slice. The times are simulated.
32 devices in a mesh: row: 8 (over y, x, core), col: 4 (over z).
Axes of the slice: x: 2, y: 2, z: 4, core: 2. Of those that a mesh axis runs over, the one named last changes fastest.
Arguments:
- homolog_embedding: bfloat16 [32, 1024, 64], P(('row', 'col')), may hold values from -6 to 6
- split_mapping_matrix: bfloat16 [64, 64], replicated, may hold values from -0.75 to 0.75
- couple_mapping_matrix: bfloat16 [1024, 128], replicated, may hold values from -1.5 to 1.5
- couple_offset_vector: bfloat16 [128], replicated, may hold values from -3 to 3
- incoming_adjoint_couple: bfloat16 [1024, 1024, 128], P('row', 'col'), may hold values from -0.29882812 to 0.29882812
Outputs:
- pair_delta_output: bfloat16 [1024, 1024, 128], P('row', 'col')
- alignment_gradient: bfloat16 [32, 1024, 64], P(('row', 'col'))
- out_weight_grad: float32 [1024, 128], replicated
All inputs are finite; a program needn't handle non-finite values.
Results may differ from a plain program's by a relative error of at most 0.015.
Values may be sent and summed in bfloat16 or wider, within the bound.
No kernel may reach another device: no remote copies, remote signals or barrier semaphores. Data moves between devices by JAX's collectives and lax.ppermute only.
A program may use at most 128 MiB of HBM per device.

v0:
```python
import math
import jax
import jax.numpy as jnp
from jax import lax
from jax.sharding import PartitionSpec as P


def standardize_features(homolog_embedding):
    mapped_halves = homolog_embedding.astype(jnp.float32)
    center = jnp.mean(mapped_halves, axis=-1, keepdims=True)
    spread = jnp.mean((mapped_halves - center) * (mapped_halves - center), axis=-1, keepdims=True)
    reciprocal_spread = lax.rsqrt(spread + 1e-05)
    return ((mapped_halves - center) * reciprocal_spread, reciprocal_spread)


def regroup(mapped_halves, outer_count, inner_count):
    shaped = mapped_halves.reshape((outer_count, inner_count, -1) + mapped_halves.shape[1:])
    return jnp.swapaxes(shaped, 0, 1).reshape(mapped_halves.shape)


def on_device(
    homolog_embedding,
    split_mapping_matrix,
    couple_mapping_matrix,
    couple_offset_vector,
    incoming_adjoint_couple,
):
    rows_count = lax.axis_size("row")
    cols_count = lax.axis_size("col")
    width = split_mapping_matrix.shape[1] // 2
    standardized_activations, reciprocal_spread = standardize_features(homolog_embedding)
    normalized_input = standardized_activations.astype(jnp.bfloat16)
    factors = jnp.dot(
        normalized_input, split_mapping_matrix, preferred_element_type=jnp.float32
    ).astype(jnp.bfloat16)
    left = factors[..., :width]
    right = factors[..., width:]
    left_all = lax.all_gather(left, "col", axis=0, tiled=True)
    left_panel = lax.all_to_all(left_all, "row", split_axis=1, concat_axis=0, tiled=True)
    right_all = lax.all_gather(right, "row", axis=0, tiled=True)
    right_panel = regroup(
        lax.all_to_all(right_all, "col", split_axis=1, concat_axis=0, tiled=True),
        cols_count,
        rows_count,
    )
    seq_total = left_panel.shape[0]
    rows_local = left_panel.shape[1]
    cols_local = right_panel.shape[1]
    channels = incoming_adjoint_couple.shape[2]
    step_rows = math.gcd(rows_local, 16)
    count = rows_local // step_rows
    left_blocks = left_panel.reshape(seq_total, count, step_rows, width).transpose(1, 0, 2, 3)
    cot_blocks = incoming_adjoint_couple.reshape(count, step_rows, cols_local, channels)
    bias_wide = couple_offset_vector.astype(jnp.float32)
    weight_back = couple_mapping_matrix.T

    def advance(carry, inputs):
        weight_sum, right_sum = carry
        left_block, cot_block = inputs
        outer = (
            jnp.einsum("sic,sje->ijce", left_block, right_panel, preferred_element_type=jnp.float32)
            / seq_total
        )
        flat = outer.astype(jnp.bfloat16).reshape(step_rows * cols_local, width * width)
        update = (
            jnp.dot(flat, couple_mapping_matrix, preferred_element_type=jnp.float32) + bias_wide
        ).astype(jnp.bfloat16)
        grad_rows = cot_block.reshape(step_rows * cols_local, channels)
        outer_grad = jnp.dot(grad_rows, weight_back, preferred_element_type=jnp.float32).astype(
            jnp.bfloat16
        )
        outer_grad = outer_grad.reshape(step_rows, cols_local, width, width)
        weight_sum = weight_sum + lax.dot_general(
            flat, grad_rows, (((0,), (0,)), ((), ())), preferred_element_type=jnp.float32
        )
        left_grad = (
            jnp.einsum("ijce,sje->sic", outer_grad, right_panel, preferred_element_type=jnp.float32)
            / seq_total
        )
        right_sum = (
            right_sum
            + jnp.einsum(
                "ijce,sic->sje", outer_grad, left_block, preferred_element_type=jnp.float32
            )
            / seq_total
        )
        return (
            (weight_sum, right_sum),
            (update.reshape(step_rows, cols_local, channels), left_grad),
        )

    start = (
        jnp.zeros((width * width, channels), jnp.float32),
        jnp.zeros((seq_total, cols_local, width), jnp.float32),
    )
    (weight_part, right_grad), (updates, left_grads) = lax.scan(
        advance, start, (left_blocks, cot_blocks)
    )
    pair_delta_output = updates.reshape(rows_local, cols_local, channels)
    left_grad = left_grads.transpose(1, 0, 2, 3).reshape(seq_total, rows_local, width)
    left_home = lax.all_to_all(
        left_grad.astype(jnp.bfloat16), "row", split_axis=0, concat_axis=1, tiled=True
    ).astype(left_grad.dtype)
    left_back = lax.psum_scatter(
        left_home.astype(jnp.bfloat16), "col", scatter_dimension=0, tiled=True
    )
    right_home = lax.all_to_all(
        regroup(right_grad, rows_count, cols_count).astype(jnp.bfloat16),
        "col",
        split_axis=0,
        concat_axis=1,
        tiled=True,
    )
    right_back = lax.psum_scatter(right_home, "row", scatter_dimension=0, tiled=True)
    factor_weight_gradient = lax.psum(weight_part, ("row", "col"))
    both = jnp.concatenate([left_back, right_back], axis=-1)
    normalized_gradient = jnp.dot(both, split_mapping_matrix.T, preferred_element_type=jnp.float32)
    first_factor = jnp.mean(normalized_gradient, axis=-1, keepdims=True)
    second_factor = jnp.mean(normalized_gradient * standardized_activations, axis=-1, keepdims=True)
    alignment_gradient = (
        reciprocal_spread
        * (normalized_gradient - first_factor - standardized_activations * second_factor)
    ).astype(jnp.bfloat16)
    return (pair_delta_output, alignment_gradient, factor_weight_gradient)


def solution(mesh):
    placed = (P(("row", "col"), None, None), P(), P(), P(), P("row", "col", None))
    return jax.shard_map(
        on_device,
        mesh=mesh,
        in_specs=placed,
        out_specs=(P("row", "col", None), P(("row", "col"), None, None), P()),
        check_vma=False,
    )
```

profile of v0, /device:TPU:0, one launch (start us, length us, event | category | flops | bytes accessed | tf_op | source)
XLA Modules:
  0.0 930.6 jit_solution(15135859743567451930)
XLA Ops:
  11.2 15.7 %all_gather.6 = bf16[4,1024,32]{1,2,0:T(8,128)(2,1)S(1)} all-gather(bf16[1,1024,32]{1,2,0:T(8,128)(2,1)S(1)} %get-tuple-element.172), channel_id=1, replica_groups=mesh['row'=8,'col'=4] {'col'}, dimensions={0}, use_global_device_ids=true | all-gather | bytes 327680 | tf_op jit(solution)/shard_map/all_gather | solution.py:38
  32.9 11.3 %all_gather.7 = bf16[8,1024,32]{1,2,0:T(8,128)(2,1)S(1)} all-gather(bf16[1,1024,32]{1,2,0:T(8,128)(2,1)S(1)} %get-tuple-element.171), channel_id=1, replica_groups=mesh['row'=8,'col'=4] {'row'}, dimensions={0}, use_global_device_ids=true | all-gather | bytes 589824 | tf_op jit(solution)/shard_map/all_gather | solution.py:40
  56.4 12.5 %all-to-all-done.1 = bf16[4,2,32768]{2,1,0:T(2,128)(2,1)S(1)} async-done(((bf16[4,2,32768]{2,1,0:T(2,128)(2,1)}), bf16[4,2,32768]{2,1,0:T(2,128)(2,1)S(1)}, u32[]{:S(2)}, u32[]{:S(2)}) %all-to-all-start.1) | async-done | bytes 524320 | tf_op jit(solution)/shard_map/all_to_all | solution.py:42
  74.7 679.0 %while.17 = (s32[]{:T(128)}, f32[1024,128]{1,0:T(8,128)S(1)}, f32[32,256,32]{1,0,2:T(8,128)S(1)}, bf16[8,16,256,128]{3,2,1,0:T(8,128)(2,1)}, bf16[8,32,16,32]{1,...) while((s32[]{:T(128)}, f32[1024,128]{1,0:T(8,128)S(1)}, ...), condition=%wide.region_3.4_spmd.clone, body=%wide.region_2.3_spmd.clone.sunk | while | flops 4041228288 | bytes 164564688 | solution.py:96
  101.6 11.4 %copy.104 = bf16[16,256,32,32]{1,0,3,2:T(8,128)(2,1)} copy(bf16[16,256,32,32]{1,2,3,0:T(8,128)(2,1)} %fusion.77) | data formatting | bytes 16777216 | tf_op jit(solution)/shard_map/while/body/eval_jaxpr/convert_element_type | solution.py:64
  113.0 12.3 %copy.105 = bf16[128,8,16,256]{3,1,2,0:T(8,128)(2,1)} copy(bf16[128,8,16,256]{3,2,1,0:T(8,128)(2,1)} %bitcast.161) | data formatting | bytes 16777216 | tf_op jit(solution)/shard_map/while
  144.8 11.4 %copy.106 = bf16[4096,1024]{0,1:T(8,128)(2,1)} copy(bf16[4096,1024]{1,0:T(8,128)(2,1)} %convolution_convert_fusion.3) | data formatting | bytes 16777216 | tf_op jit(solution)/shard_map/while/body/eval_jaxpr/convert_element_type | solution.py:69
  183.9 11.4 %copy.104 = bf16[16,256,32,32]{1,0,3,2:T(8,128)(2,1)} copy(bf16[16,256,32,32]{1,2,3,0:T(8,128)(2,1)} %fusion.77) | data formatting | bytes 16777216 | tf_op jit(solution)/shard_map/while/body/eval_jaxpr/convert_element_type | solution.py:64
  195.3 12.3 %copy.105 = bf16[128,8,16,256]{3,1,2,0:T(8,128)(2,1)} copy(bf16[128,8,16,256]{3,2,1,0:T(8,128)(2,1)} %bitcast.161) | data formatting | bytes 16777216 | tf_op jit(solution)/shard_map/while
  227.1 11.4 %copy.106 = bf16[4096,1024]{0,1:T(8,128)(2,1)} copy(bf16[4096,1024]{1,0:T(8,128)(2,1)} %convolution_convert_fusion.3) | data formatting | bytes 16777216 | tf_op jit(solution)/shard_map/while/body/eval_jaxpr/convert_element_type | solution.py:69
  266.3 11.4 %copy.104 = bf16[16,256,32,32]{1,0,3,2:T(8,128)(2,1)} copy(bf16[16,256,32,32]{1,2,3,0:T(8,128)(2,1)} %fusion.77) | data formatting | bytes 16777216 | tf_op jit(solution)/shard_map/while/body/eval_jaxpr/convert_element_type | solution.py:64
  277.7 12.3 %copy.105 = bf16[128,8,16,256]{3,1,2,0:T(8,128)(2,1)} copy(bf16[128,8,16,256]{3,2,1,0:T(8,128)(2,1)} %bitcast.161) | data formatting | bytes 16777216 | tf_op jit(solution)/shard_map/while
  309.5 11.4 %copy.106 = bf16[4096,1024]{0,1:T(8,128)(2,1)} copy(bf16[4096,1024]{1,0:T(8,128)(2,1)} %convolution_convert_fusion.3) | data formatting | bytes 16777216 | tf_op jit(solution)/shard_map/while/body/eval_jaxpr/convert_element_type | solution.py:69
  320.9 9.7 %copy.107 = bf16[128,8,16,256]{3,2,1,0:T(8,128)(2,1)} copy(bf16[128,8,16,256]{3,1,2,0:T(8,128)(2,1)} %bitcast.162) | data formatting | bytes 16777216 | tf_op jit(solution)/shard_map/while
  348.6 11.4 %copy.104 = bf16[16,256,32,32]{1,0,3,2:T(8,128)(2,1)} copy(bf16[16,256,32,32]{1,2,3,0:T(8,128)(2,1)} %fusion.77) | data formatting | bytes 16777216 | tf_op jit(solution)/shard_map/while/body/eval_jaxpr/convert_element_type | solution.py:64
  360.0 12.3 %copy.105 = bf16[128,8,16,256]{3,1,2,0:T(8,128)(2,1)} copy(bf16[128,8,16,256]{3,2,1,0:T(8,128)(2,1)} %bitcast.161) | data formatting | bytes 16777216 | tf_op jit(solution)/shard_map/while
  391.8 11.4 %copy.106 = bf16[4096,1024]{0,1:T(8,128)(2,1)} copy(bf16[4096,1024]{1,0:T(8,128)(2,1)} %convolution_convert_fusion.3) | data formatting | bytes 16777216 | tf_op jit(solution)/shard_map/while/body/eval_jaxpr/convert_element_type | solution.py:69
  430.9 11.4 %copy.104 = bf16[16,256,32,32]{1,0,3,2:T(8,128)(2,1)} copy(bf16[16,256,32,32]{1,2,3,0:T(8,128)(2,1)} %fusion.77) | data formatting | bytes 16777216 | tf_op jit(solution)/shard_map/while/body/eval_jaxpr/convert_element_type | solution.py:64
  442.3 12.3 %copy.105 = bf16[128,8,16,256]{3,1,2,0:T(8,128)(2,1)} copy(bf16[128,8,16,256]{3,2,1,0:T(8,128)(2,1)} %bitcast.161) | data formatting | bytes 16777216 | tf_op jit(solution)/shard_map/while
  474.1 11.4 %copy.106 = bf16[4096,1024]{0,1:T(8,128)(2,1)} copy(bf16[4096,1024]{1,0:T(8,128)(2,1)} %convolution_convert_fusion.3) | data formatting | bytes 16777216 | tf_op jit(solution)/shard_map/while/body/eval_jaxpr/convert_element_type | solution.py:69
  513.2 11.4 %copy.104 = bf16[16,256,32,32]{1,0,3,2:T(8,128)(2,1)} copy(bf16[16,256,32,32]{1,2,3,0:T(8,128)(2,1)} %fusion.77) | data formatting | bytes 16777216 | tf_op jit(solution)/shard_map/while/body/eval_jaxpr/convert_element_type | solution.py:64
  524.6 12.3 %copy.105 = bf16[128,8,16,256]{3,1,2,0:T(8,128)(2,1)} copy(bf16[128,8,16,256]{3,2,1,0:T(8,128)(2,1)} %bitcast.161) | data formatting | bytes 16777216 | tf_op jit(solution)/shard_map/while
  556.4 11.4 %copy.106 = bf16[4096,1024]{0,1:T(8,128)(2,1)} copy(bf16[4096,1024]{1,0:T(8,128)(2,1)} %convolution_convert_fusion.3) | data formatting | bytes 16777216 | tf_op jit(solution)/shard_map/while/body/eval_jaxpr/convert_element_type | solution.py:69
  595.6 11.4 %copy.104 = bf16[16,256,32,32]{1,0,3,2:T(8,128)(2,1)} copy(bf16[16,256,32,32]{1,2,3,0:T(8,128)(2,1)} %fusion.77) | data formatting | bytes 16777216 | tf_op jit(solution)/shard_map/while/body/eval_jaxpr/convert_element_type | solution.py:64
  606.9 12.3 %copy.105 = bf16[128,8,16,256]{3,1,2,0:T(8,128)(2,1)} copy(bf16[128,8,16,256]{3,2,1,0:T(8,128)(2,1)} %bitcast.161) | data formatting | bytes 16777216 | tf_op jit(solution)/shard_map/while
  638.7 11.4 %copy.106 = bf16[4096,1024]{0,1:T(8,128)(2,1)} copy(bf16[4096,1024]{1,0:T(8,128)(2,1)} %convolution_convert_fusion.3) | data formatting | bytes 16777216 | tf_op jit(solution)/shard_map/while/body/eval_jaxpr/convert_element_type | solution.py:69
  677.9 11.4 %copy.104 = bf16[16,256,32,32]{1,0,3,2:T(8,128)(2,1)} copy(bf16[16,256,32,32]{1,2,3,0:T(8,128)(2,1)} %fusion.77) | data formatting | bytes 16777216 | tf_op jit(solution)/shard_map/while/body/eval_jaxpr/convert_element_type | solution.py:64
  689.3 12.3 %copy.105 = bf16[128,8,16,256]{3,1,2,0:T(8,128)(2,1)} copy(bf16[128,8,16,256]{3,2,1,0:T(8,128)(2,1)} %bitcast.161) | data formatting | bytes 16777216 | tf_op jit(solution)/shard_map/while
  721.1 11.4 %copy.106 = bf16[4096,1024]{0,1:T(8,128)(2,1)} copy(bf16[4096,1024]{1,0:T(8,128)(2,1)} %convolution_convert_fusion.3) | data formatting | bytes 16777216 | tf_op jit(solution)/shard_map/while/body/eval_jaxpr/convert_element_type | solution.py:69
  772.8 16.1 %all-to-all-done.3 = bf16[32,256,32]{1,2,0:T(8,128)(2,1)S(1)} async-done(((bf16[32,256,32]{1,2,0:T(8,128)(2,1)}), bf16[32,256,32]{1,2,0:T(8,128)(2,1)S(1)}, u32[]{:S(2)}, u32[]{:S(2)}) %all-to-all-start.3) | async-done | bytes 524320 | tf_op jit(solution)/shard_map/all_to_all | solution.py:107
  794.2 37.3 %reduce-scatter.5.cloned.1.call-done = bf16[1,1024,32]{1,2,0:T(8,128)(2,1)} async-done(((bf16[8,1024,32]{1,2,0:T(8,128)(2,1)}), bf16[1,1024,32]{1,2,0:T(8,128)(2,1)}) %reduce-scatter.5.cloned.1.call-update) | async-done | bytes 65552 | tf_op jit(solution)/shard_map/reduce_scatter | solution.py:114
  833.4 87.6 %all-reduce.2.cloned.1.call-done = f32[1024,128]{1,0:T(8,128)} async-done(((f32[1024,128]{1,0:T(8,128)}), f32[1024,128]{1,0:T(8,128)}) %all-reduce.2.cloned.1.call-update) | async-done | bytes 524304 | tf_op jit(solution)/shard_map/psum | solution.py:115
  (192 shorter events, 423.2 us)
Async XLA Ops:
  8.0 45.9 %copy-start.5 = (bf16[1024,128]{1,0:T(8,128)(2,1)S(1)}, bf16[1024,128]{1,0:T(8,128)(2,1)}, u32[]{:S(2)}) copy-start(bf16[1024,128]{1,0:T(8,128)(2,1)} %param.9) | copy-start | bytes 786436
  26.8 27.3 %copy-start.11 = (bf16[128]{0:T(256)(128)(2,1)S(1)}, bf16[128]{0:T(256)(128)(2,1)}, u32[]{:S(2)}) copy-start(bf16[128]{0:T(256)(128)(2,1)} %param.10) | copy-start | bytes 772
  29.2 19.6 %all-to-all-start = ((bf16[8,2,8192]{2,1,0:T(2,128)(2,1)}), bf16[8,2,8192]{2,1,0:T(2,128)(2,1)S(1)}, u32[]{:S(2)}, u32[]{:S(2)}) async-start(bf16[8,2,8192]{2,1,0:T(2,128)(2,1)} %reshape.107), calls=%async_computation | async-start | bytes 524288 | tf_op jit(solution)/shard_map/all_to_all | solution.py:39
  48.8 20.2 %all-to-all-start.1 = ((bf16[4,2,32768]{2,1,0:T(2,128)(2,1)}), bf16[4,2,32768]{2,1,0:T(2,128)(2,1)S(1)}, u32[]{:S(2)}, u32[]{:S(2)}) async-start(bf16[4,2,32768]{2,1,0:T(2,128)(2,1)} %reshape.109), calls=%async_computation.1 | async-start | bytes 1048576 | tf_op jit(solution)/shard_map/all_to_all | solution.py:42
  55.1 19.6 %copy-start.3 = (f32[1024,128]{1,0:T(8,128)S(1)}, f32[1024,128]{1,0:T(8,128)}, u32[]{:S(2)}) copy-start(f32[1024,128]{1,0:T(8,128)} %custom-call) | copy-start | bytes 1572868
  113.0 12.3 %copy-start.6 = (bf16[1024,128]{1,0:T(8,128)(2,1)S(1)}, bf16[1024,128]{1,0:T(8,128)(2,1)}, u32[]{:S(2)}) copy-start(bf16[1024,128]{1,0:T(8,128)(2,1)} %get-tuple-element.283) | copy-start | bytes 786436 | tf_op jit(solution)/shard_map/while
  113.0 12.3 %copy-start.12 = (f32[128]{0:T(128)S(1)}, f32[128]{0:T(128)}, u32[]{:S(2)}) copy-start(f32[128]{0:T(128)} %get-tuple-element.284) | copy-start | bytes 1540 | tf_op jit(solution)/shard_map/while
  165.9 8.4 copy-start.1
  195.3 12.3 %copy-start.6 = (bf16[1024,128]{1,0:T(8,128)(2,1)S(1)}, bf16[1024,128]{1,0:T(8,128)(2,1)}, u32[]{:S(2)}) copy-start(bf16[1024,128]{1,0:T(8,128)(2,1)} %get-tuple-element.283) | copy-start | bytes 786436 | tf_op jit(solution)/shard_map/while
  195.3 12.3 %copy-start.12 = (f32[128]{0:T(128)S(1)}, f32[128]{0:T(128)}, u32[]{:S(2)}) copy-start(f32[128]{0:T(128)} %get-tuple-element.284) | copy-start | bytes 1540 | tf_op jit(solution)/shard_map/while
  248.2 8.4 copy-start.1
  277.7 12.3 %copy-start.6 = (bf16[1024,128]{1,0:T(8,128)(2,1)S(1)}, bf16[1024,128]{1,0:T(8,128)(2,1)}, u32[]{:S(2)}) copy-start(bf16[1024,128]{1,0:T(8,128)(2,1)} %get-tuple-element.283) | copy-start | bytes 786436 | tf_op jit(solution)/shard_map/while
  277.7 12.3 %copy-start.12 = (f32[128]{0:T(128)S(1)}, f32[128]{0:T(128)}, u32[]{:S(2)}) copy-start(f32[128]{0:T(128)} %get-tuple-element.284) | copy-start | bytes 1540 | tf_op jit(solution)/shard_map/while
  360.0 12.3 %copy-start.6 = (bf16[1024,128]{1,0:T(8,128)(2,1)S(1)}, bf16[1024,128]{1,0:T(8,128)(2,1)}, u32[]{:S(2)}) copy-start(bf16[1024,128]{1,0:T(8,128)(2,1)} %get-tuple-element.283) | copy-start | bytes 786436 | tf_op jit(solution)/shard_map/while
  360.0 12.3 %copy-start.12 = (f32[128]{0:T(128)S(1)}, f32[128]{0:T(128)}, u32[]{:S(2)}) copy-start(f32[128]{0:T(128)} %get-tuple-element.284) | copy-start | bytes 1540 | tf_op jit(solution)/shard_map/while
  442.3 12.3 %copy-start.6 = (bf16[1024,128]{1,0:T(8,128)(2,1)S(1)}, bf16[1024,128]{1,0:T(8,128)(2,1)}, u32[]{:S(2)}) copy-start(bf16[1024,128]{1,0:T(8,128)(2,1)} %get-tuple-element.283) | copy-start | bytes 786436 | tf_op jit(solution)/shard_map/while
  442.3 12.3 %copy-start.12 = (f32[128]{0:T(128)S(1)}, f32[128]{0:T(128)}, u32[]{:S(2)}) copy-start(f32[128]{0:T(128)} %get-tuple-element.284) | copy-start | bytes 1540 | tf_op jit(solution)/shard_map/while
  524.6 12.3 %copy-start.6 = (bf16[1024,128]{1,0:T(8,128)(2,1)S(1)}, bf16[1024,128]{1,0:T(8,128)(2,1)}, u32[]{:S(2)}) copy-start(bf16[1024,128]{1,0:T(8,128)(2,1)} %get-tuple-element.283) | copy-start | bytes 786436 | tf_op jit(solution)/shard_map/while
  524.6 12.3 %copy-start.12 = (f32[128]{0:T(128)S(1)}, f32[128]{0:T(128)}, u32[]{:S(2)}) copy-start(f32[128]{0:T(128)} %get-tuple-element.284) | copy-start | bytes 1540 | tf_op jit(solution)/shard_map/while
  606.9 12.3 %copy-start.6 = (bf16[1024,128]{1,0:T(8,128)(2,1)S(1)}, bf16[1024,128]{1,0:T(8,128)(2,1)}, u32[]{:S(2)}) copy-start(bf16[1024,128]{1,0:T(8,128)(2,1)} %get-tuple-element.283) | copy-start | bytes 786436 | tf_op jit(solution)/shard_map/while
  606.9 12.3 %copy-start.12 = (f32[128]{0:T(128)S(1)}, f32[128]{0:T(128)}, u32[]{:S(2)}) copy-start(f32[128]{0:T(128)} %get-tuple-element.284) | copy-start | bytes 1540 | tf_op jit(solution)/shard_map/while
  689.2 12.3 %copy-start.6 = (bf16[1024,128]{1,0:T(8,128)(2,1)S(1)}, bf16[1024,128]{1,0:T(8,128)(2,1)}, u32[]{:S(2)}) copy-start(bf16[1024,128]{1,0:T(8,128)(2,1)} %get-tuple-element.283) | copy-start | bytes 786436 | tf_op jit(solution)/shard_map/while
  689.2 12.3 %copy-start.12 = (f32[128]{0:T(128)S(1)}, f32[128]{0:T(128)}, u32[]{:S(2)}) copy-start(f32[128]{0:T(128)} %get-tuple-element.284) | copy-start | bytes 1540 | tf_op jit(solution)/shard_map/while
  753.7 36.1 %copy-start.4 = (f32[1024,128]{1,0:T(8,128)}, f32[1024,128]{1,0:T(8,128)S(1)}, u32[]{:S(2)}) copy-start(f32[1024,128]{1,0:T(8,128)S(1)} %get-tuple-element.66) | copy-start | bytes 1572868
  753.7 77.8 %copy-start.2 = (bf16[1,1024,64]{1,2,0:T(8,128)(2,1)S(1)}, bf16[1,1024,64]{1,2,0:T(8,128)(2,1)}, u32[]{:S(2)}) copy-start(bf16[1,1024,64]{1,2,0:T(8,128)(2,1)} %param.7) | copy-start | bytes 393220
  753.7 77.8 %copy-start.8 = (f32[1024]{0:T(1024)S(1)}, f32[1024]{0:T(1024)}, u32[]{:S(2)}) copy-start(f32[1024]{0:T(1024)} %copy-done.7) | copy-start | bytes 12292
  753.8 77.8 %copy-start.10 = (f32[1024]{0:T(1024)S(1)}, f32[1024]{0:T(1024)}, u32[]{:S(2)}) copy-start(f32[1024]{0:T(1024)} %copy-done.9) | copy-start | bytes 12292
  758.2 10.3 %all-to-all-start.2 = ((bf16[32,128,32]{1,2,0:T(8,128)(2,1)}), bf16[32,128,32]{1,2,0:T(8,128)(2,1)S(1)}, u32[]{:S(2)}, u32[]{:S(2)}) async-start(bf16[32,128,32]{1,2,0:T(8,128)(2,1)} %copy.67), calls=%async_computation.2 | async-start | bytes 524288 | tf_op jit(solution)/shard_map/all_to_all | solution.py:101
  768.4 20.5 %all-to-all-start.3 = ((bf16[32,256,32]{1,2,0:T(8,128)(2,1)}), bf16[32,256,32]{1,2,0:T(8,128)(2,1)S(1)}, u32[]{:S(2)}, u32[]{:S(2)}) async-start(bf16[32,256,32]{1,2,0:T(8,128)(2,1)} %bitcast.20), calls=%async_computation.4 | async-start | bytes 1048576 | tf_op jit(solution)/shard_map/all_to_all | solution.py:107
  771.9 22.3 %reduce-scatter.3.cloned.1.call-start = ((), (), s32[]{:S(2)}) async-start(), calls=%async_computation.6 | async-start | bytes 327680 | tf_op jit(solution)/shard_map/reduce_scatter | solution.py:104
  772.8 58.8 %reduce-scatter.5.cloned.1.call-start = ((), (), s32[]{:S(2)}) async-start(), calls=%async_computation.7 | async-start | bytes 589824 | tf_op jit(solution)/shard_map/reduce_scatter | solution.py:114
  789.8 131.2 %all-reduce.2.cloned.1.call-start = ((), (), s32[]{:S(2)}) async-start(), calls=%async_computation.8 | async-start | bytes 1048576 | tf_op jit(solution)/shard_map/psum | solution.py:115
  (9 other events, 55.6 us)
Sparse Core Ops, SparseCore 0:
  775.0 19.1 reduce-scatter.2
  797.9 33.6 reduce-scatter.4
Sparse Core Ops, SparseCore 1:
  795.5 125.4 all-reduce.1
where the time goes:
time: 940 us; the launch traced here: 931 us
  local copies, waits for them, and re-layouts  410 us (44%)
  matrix products  274 us (29%)
  waiting for transfers between devices  163 us (17%)
  blocking collectives  26.9 us (3%)
  loops' own time  20.7 us (2%)
  between operations  16.1 us (2%)
  starting transfers between devices  15.9 us (2%)
    while x64, local copies, waits for them, and re-layouts  176 us
    convert_element_type x8, local copies, waits for them, and re-layouts, advance(): jnp.dot(grad_rows, weight_back, preferred_element_type=jnp.float32)  91.1 us
    convert_element_type x8, local copies, waits for them, and re-layouts, advance(): outer.astype(jnp.bfloat16).reshape(step_rows * cols_local, width * width)  91 us
    psum x1, waiting for transfers between devices, on_device(): factor_weight_gradient = lax.psum(weight_part, ('row', 'col'))  87.6 us
    dot_general x8, matrix products, advance(): jnp.einsum('ijce,sic->sje', outer_grad, left_block, preferred_element_typ...  67 us
    dot_general x8, matrix products, advance(): lax.dot_general(flat, grad_rows, (((0,), (0,)), ((), ())), preferred_elem...  46.3 us
    dot_general x8, matrix products, advance(): jnp.dot(flat, couple_mapping_matrix, preferred_element_type=jnp.float32)  46.1 us
    dot_general x8, matrix products, advance(): jnp.dot(grad_rows, weight_back, preferred_element_type=jnp.float32)  44.5 us
  transfers between devices with their start and end apart: 7, of which 6 were waited for; matrix products, arithmetic and copies ran while one was open for 1% of the time, Pallas kernels for 0%

commit v1 on v0

--- a/solution.py
+++ b/solution.py
@@ -112,7 +112,7 @@
         tiled=True,
     )
     right_back = lax.psum_scatter(right_home, "row", scatter_dimension=0, tiled=True)
-    factor_weight_gradient = lax.psum(weight_part, ("row", "col"))
+    factor_weight_gradient = lax.psum(lax.psum(weight_part, "col"), "row")
     both = jnp.concatenate([left_back, right_back], axis=-1)
     normalized_gradient = jnp.dot(both, split_mapping_matrix.T, preferred_element_type=jnp.float32)
     first_factor = jnp.mean(normalized_gradient, axis=-1, keepdims=True)

time: 940 us -> 927 us (0.986)
  waiting for transfers between devices: 163 us -> 152 us
    psum x1 -> x2, waiting for transfers between devices: 87.6 us -> 56 us  [on_device(): factor_weight_gradient = lax.psum(lax.psum(weight_part, 'col'), 'row')]
    reduce_scatter x1, waiting for transfers between devices: 3.85 us -> 20.6 us  [on_device(): lax.psum_scatter(left_home.astype(jnp.bfloat16), 'col', scatter_dimension...]
  transfers between devices with their start and end apart: 7 -> 8, of which waited for: 6 -> 6; matrix products, arithmetic and copies ran while one was open for 1% -> 2% of each run, Pallas kernels for 0% -> 0%
where the time goes in v1:
time: 927 us; the launch traced here: 919 us
  local copies, waits for them, and re-layouts  411 us (44%)
  matrix products  274 us (30%)
  waiting for transfers between devices  152 us (16%)
  blocking collectives  26.9 us (3%)
  loops' own time  20.7 us (2%)
  starting transfers between devices  15.9 us (2%)
  between operations  14.4 us (2%)
    while x64, local copies, waits for them, and re-layouts  176 us
    convert_element_type x8, local copies, waits for them, and re-layouts, advance(): jnp.dot(grad_rows, weight_back, preferred_element_type=jnp.float32)  91.1 us
    convert_element_type x8, local copies, waits for them, and re-layouts, advance(): outer.astype(jnp.bfloat16).reshape(step_rows * cols_local, width * width)  91 us
    dot_general x8, matrix products, advance(): jnp.einsum('ijce,sic->sje', outer_grad, left_block, preferred_element_typ...  67 us
    psum x2, waiting for transfers between devices, on_device(): factor_weight_gradient = lax.psum(lax.psum(weight_part, 'col'), 'row')  56 us
    dot_general x8, matrix products, advance(): lax.dot_general(flat, grad_rows, (((0,), (0,)), ((), ())), preferred_elem...  46.3 us
    dot_general x8, matrix products, advance(): jnp.dot(flat, couple_mapping_matrix, preferred_element_type=jnp.float32)  46.1 us
    dot_general x8, matrix products, advance(): jnp.dot(grad_rows, weight_back, preferred_element_type=jnp.float32)  44.5 us
  transfers between devices with their start and end apart: 8, of which 6 were waited for; matrix products, arithmetic and copies ran while one was open for 2% of the time, Pallas kernels for 0%

profile of v1, /device:TPU:0, one launch (start us, length us, event | category | flops | bytes accessed | tf_op | source)
XLA Modules:
  0.0 918.6 jit_solution(17376376785419457085)
XLA Ops:
  10.4 15.7 %all_gather.6 = bf16[4,1024,32]{1,2,0:T(8,128)(2,1)S(1)} all-gather(bf16[1,1024,32]{1,2,0:T(8,128)(2,1)S(1)} %get-tuple-element.172), channel_id=1, replica_groups=mesh['row'=8,'col'=4] {'col'}, dimensions={0}, use_global_device_ids=true | all-gather | bytes 327680 | tf_op jit(solution)/shard_map/all_gather | solution.py:38
  32.1 11.3 %all_gather.7 = bf16[8,1024,32]{1,2,0:T(8,128)(2,1)S(1)} all-gather(bf16[1,1024,32]{1,2,0:T(8,128)(2,1)S(1)} %get-tuple-element.171), channel_id=1, replica_groups=mesh['row'=8,'col'=4] {'row'}, dimensions={0}, use_global_device_ids=true | all-gather | bytes 589824 | tf_op jit(solution)/shard_map/all_gather | solution.py:40
  55.6 12.5 %all-to-all-done.1 = bf16[4,2,32768]{2,1,0:T(2,128)(2,1)S(1)} async-done(((bf16[4,2,32768]{2,1,0:T(2,128)(2,1)}), bf16[4,2,32768]{2,1,0:T(2,128)(2,1)S(1)}, u32[]{:S(2)}, u32[]{:S(2)}) %all-to-all-start.1) | async-done | bytes 524320 | tf_op jit(solution)/shard_map/all_to_all | solution.py:42
  73.9 679.0 %while.17 = (s32[]{:T(128)}, f32[1024,128]{1,0:T(8,128)S(1)}, f32[32,256,32]{1,0,2:T(8,128)S(1)}, bf16[8,16,256,128]{3,2,1,0:T(8,128)(2,1)}, bf16[8,32,16,32]{1,...) while((s32[]{:T(128)}, f32[1024,128]{1,0:T(8,128)S(1)}, ...), condition=%wide.region_3.4_spmd.clone, body=%wide.region_2.3_spmd.clone.sunk | while | flops 4041228288 | bytes 164564688 | solution.py:96
  100.8 11.4 %copy.104 = bf16[16,256,32,32]{1,0,3,2:T(8,128)(2,1)} copy(bf16[16,256,32,32]{1,2,3,0:T(8,128)(2,1)} %fusion.77) | data formatting | bytes 16777216 | tf_op jit(solution)/shard_map/while/body/eval_jaxpr/convert_element_type | solution.py:64
  112.2 12.3 %copy.105 = bf16[128,8,16,256]{3,1,2,0:T(8,128)(2,1)} copy(bf16[128,8,16,256]{3,2,1,0:T(8,128)(2,1)} %bitcast.161) | data formatting | bytes 16777216 | tf_op jit(solution)/shard_map/while
  144.0 11.4 %copy.106 = bf16[4096,1024]{0,1:T(8,128)(2,1)} copy(bf16[4096,1024]{1,0:T(8,128)(2,1)} %convolution_convert_fusion.3) | data formatting | bytes 16777216 | tf_op jit(solution)/shard_map/while/body/eval_jaxpr/convert_element_type | solution.py:69
  183.1 11.4 %copy.104 = bf16[16,256,32,32]{1,0,3,2:T(8,128)(2,1)} copy(bf16[16,256,32,32]{1,2,3,0:T(8,128)(2,1)} %fusion.77) | data formatting | bytes 16777216 | tf_op jit(solution)/shard_map/while/body/eval_jaxpr/convert_element_type | solution.py:64
  194.5 12.3 %copy.105 = bf16[128,8,16,256]{3,1,2,0:T(8,128)(2,1)} copy(bf16[128,8,16,256]{3,2,1,0:T(8,128)(2,1)} %bitcast.161) | data formatting | bytes 16777216 | tf_op jit(solution)/shard_map/while
  226.3 11.4 %copy.106 = bf16[4096,1024]{0,1:T(8,128)(2,1)} copy(bf16[4096,1024]{1,0:T(8,128)(2,1)} %convolution_convert_fusion.3) | data formatting | bytes 16777216 | tf_op jit(solution)/shard_map/while/body/eval_jaxpr/convert_element_type | solution.py:69
  265.5 11.4 %copy.104 = bf16[16,256,32,32]{1,0,3,2:T(8,128)(2,1)} copy(bf16[16,256,32,32]{1,2,3,0:T(8,128)(2,1)} %fusion.77) | data formatting | bytes 16777216 | tf_op jit(solution)/shard_map/while/body/eval_jaxpr/convert_element_type | solution.py:64
  276.8 12.3 %copy.105 = bf16[128,8,16,256]{3,1,2,0:T(8,128)(2,1)} copy(bf16[128,8,16,256]{3,2,1,0:T(8,128)(2,1)} %bitcast.161) | data formatting | bytes 16777216 | tf_op jit(solution)/shard_map/while
  308.6 11.4 %copy.106 = bf16[4096,1024]{0,1:T(8,128)(2,1)} copy(bf16[4096,1024]{1,0:T(8,128)(2,1)} %convolution_convert_fusion.3) | data formatting | bytes 16777216 | tf_op jit(solution)/shard_map/while/body/eval_jaxpr/convert_element_type | solution.py:69
  347.8 11.4 %copy.104 = bf16[16,256,32,32]{1,0,3,2:T(8,128)(2,1)} copy(bf16[16,256,32,32]{1,2,3,0:T(8,128)(2,1)} %fusion.77) | data formatting | bytes 16777216 | tf_op jit(solution)/shard_map/while/body/eval_jaxpr/convert_element_type | solution.py:64
  359.1 12.3 %copy.105 = bf16[128,8,16,256]{3,1,2,0:T(8,128)(2,1)} copy(bf16[128,8,16,256]{3,2,1,0:T(8,128)(2,1)} %bitcast.161) | data formatting | bytes 16777216 | tf_op jit(solution)/shard_map/while
  390.9 11.4 %copy.106 = bf16[4096,1024]{0,1:T(8,128)(2,1)} copy(bf16[4096,1024]{1,0:T(8,128)(2,1)} %convolution_convert_fusion.3) | data formatting | bytes 16777216 | tf_op jit(solution)/shard_map/while/body/eval_jaxpr/convert_element_type | solution.py:69
  430.1 11.4 %copy.104 = bf16[16,256,32,32]{1,0,3,2:T(8,128)(2,1)} copy(bf16[16,256,32,32]{1,2,3,0:T(8,128)(2,1)} %fusion.77) | data formatting | bytes 16777216 | tf_op jit(solution)/shard_map/while/body/eval_jaxpr/convert_element_type | solution.py:64
  441.5 12.3 %copy.105 = bf16[128,8,16,256]{3,1,2,0:T(8,128)(2,1)} copy(bf16[128,8,16,256]{3,2,1,0:T(8,128)(2,1)} %bitcast.161) | data formatting | bytes 16777216 | tf_op jit(solution)/shard_map/while
  473.3 11.4 %copy.106 = bf16[4096,1024]{0,1:T(8,128)(2,1)} copy(bf16[4096,1024]{1,0:T(8,128)(2,1)} %convolution_convert_fusion.3) | data formatting | bytes 16777216 | tf_op jit(solution)/shard_map/while/body/eval_jaxpr/convert_element_type | solution.py:69
  512.4 11.4 %copy.104 = bf16[16,256,32,32]{1,0,3,2:T(8,128)(2,1)} copy(bf16[16,256,32,32]{1,2,3,0:T(8,128)(2,1)} %fusion.77) | data formatting | bytes 16777216 | tf_op jit(solution)/shard_map/while/body/eval_jaxpr/convert_element_type | solution.py:64
  523.8 12.3 %copy.105 = bf16[128,8,16,256]{3,1,2,0:T(8,128)(2,1)} copy(bf16[128,8,16,256]{3,2,1,0:T(8,128)(2,1)} %bitcast.161) | data formatting | bytes 16777216 | tf_op jit(solution)/shard_map/while
  555.6 11.4 %copy.106 = bf16[4096,1024]{0,1:T(8,128)(2,1)} copy(bf16[4096,1024]{1,0:T(8,128)(2,1)} %convolution_convert_fusion.3) | data formatting | bytes 16777216 | tf_op jit(solution)/shard_map/while/body/eval_jaxpr/convert_element_type | solution.py:69
  594.7 11.4 %copy.104 = bf16[16,256,32,32]{1,0,3,2:T(8,128)(2,1)} copy(bf16[16,256,32,32]{1,2,3,0:T(8,128)(2,1)} %fusion.77) | data formatting | bytes 16777216 | tf_op jit(solution)/shard_map/while/body/eval_jaxpr/convert_element_type | solution.py:64
  606.1 12.3 %copy.105 = bf16[128,8,16,256]{3,1,2,0:T(8,128)(2,1)} copy(bf16[128,8,16,256]{3,2,1,0:T(8,128)(2,1)} %bitcast.161) | data formatting | bytes 16777216 | tf_op jit(solution)/shard_map/while
  637.9 11.4 %copy.106 = bf16[4096,1024]{0,1:T(8,128)(2,1)} copy(bf16[4096,1024]{1,0:T(8,128)(2,1)} %convolution_convert_fusion.3) | data formatting | bytes 16777216 | tf_op jit(solution)/shard_map/while/body/eval_jaxpr/convert_element_type | solution.py:69
  677.0 11.4 %copy.104 = bf16[16,256,32,32]{1,0,3,2:T(8,128)(2,1)} copy(bf16[16,256,32,32]{1,2,3,0:T(8,128)(2,1)} %fusion.77) | data formatting | bytes 16777216 | tf_op jit(solution)/shard_map/while/body/eval_jaxpr/convert_element_type | solution.py:64
  688.4 12.3 %copy.105 = bf16[128,8,16,256]{3,1,2,0:T(8,128)(2,1)} copy(bf16[128,8,16,256]{3,2,1,0:T(8,128)(2,1)} %bitcast.161) | data formatting | bytes 16777216 | tf_op jit(solution)/shard_map/while
  720.2 11.4 %copy.106 = bf16[4096,1024]{0,1:T(8,128)(2,1)} copy(bf16[4096,1024]{1,0:T(8,128)(2,1)} %convolution_convert_fusion.3) | data formatting | bytes 16777216 | tf_op jit(solution)/shard_map/while/body/eval_jaxpr/convert_element_type | solution.py:69
  772.6 21.3 %all-to-all-done.3 = bf16[32,256,32]{1,2,0:T(8,128)(2,1)S(1)} async-done(((bf16[32,256,32]{1,2,0:T(8,128)(2,1)}), bf16[32,256,32]{1,2,0:T(8,128)(2,1)S(1)}, u32[]{:S(2)}, u32[]{:S(2)}) %all-to-all-start.3) | async-done | bytes 524320 | tf_op jit(solution)/shard_map/all_to_all | solution.py:107
  795.3 20.6 %reduce-scatter.3.cloned.1.call-done = bf16[1,1024,32]{1,2,0:T(8,128)(2,1)} async-done(((bf16[4,1024,32]{1,2,0:T(8,128)(2,1)}), bf16[1,1024,32]{1,2,0:T(8,128)(2,1)}) %reduce-scatter.3.cloned.1.call-update) | async-done | bytes 65552 | tf_op jit(solution)/shard_map/reduce_scatter | solution.py:104
  816.0 36.1 %reduce-scatter.5.cloned.1.call-done = bf16[1,1024,32]{1,2,0:T(8,128)(2,1)} async-done(((bf16[8,1024,32]{1,2,0:T(8,128)(2,1)}), bf16[1,1024,32]{1,2,0:T(8,128)(2,1)}) %reduce-scatter.5.cloned.1.call-update) | async-done | bytes 65552 | tf_op jit(solution)/shard_map/reduce_scatter | solution.py:114
  853.8 56.0 %all-reduce.5.cloned.1.call-done = f32[1024,128]{1,0:T(8,128)} async-done(((f32[1024,128]{1,0:T(8,128)}), f32[1024,128]{1,0:T(8,128)}) %all-reduce.5.cloned.1.call-update) | async-done | bytes 524304 | tf_op jit(solution)/shard_map/psum | solution.py:115
  (195 shorter events, 429.6 us)
Async XLA Ops:
  7.2 46.0 %copy-start.5 = (bf16[1024,128]{1,0:T(8,128)(2,1)S(1)}, bf16[1024,128]{1,0:T(8,128)(2,1)}, u32[]{:S(2)}) copy-start(bf16[1024,128]{1,0:T(8,128)(2,1)} %param.9) | copy-start | bytes 786436
  26.0 27.3 %copy-start.11 = (bf16[128]{0:T(256)(128)(2,1)S(1)}, bf16[128]{0:T(256)(128)(2,1)}, u32[]{:S(2)}) copy-start(bf16[128]{0:T(256)(128)(2,1)} %param.10) | copy-start | bytes 772
  28.4 19.6 %all-to-all-start = ((bf16[8,2,8192]{2,1,0:T(2,128)(2,1)}), bf16[8,2,8192]{2,1,0:T(2,128)(2,1)S(1)}, u32[]{:S(2)}, u32[]{:S(2)}) async-start(bf16[8,2,8192]{2,1,0:T(2,128)(2,1)} %reshape.107), calls=%async_computation | async-start | bytes 524288 | tf_op jit(solution)/shard_map/all_to_all | solution.py:39
  47.9 20.2 %all-to-all-start.1 = ((bf16[4,2,32768]{2,1,0:T(2,128)(2,1)}), bf16[4,2,32768]{2,1,0:T(2,128)(2,1)S(1)}, u32[]{:S(2)}, u32[]{:S(2)}) async-start(bf16[4,2,32768]{2,1,0:T(2,128)(2,1)} %reshape.109), calls=%async_computation.1 | async-start | bytes 1048576 | tf_op jit(solution)/shard_map/all_to_all | solution.py:42
  53.1 741.7 %all-reduce.3.cloned.1.call-start = ((), (), s32[]{:S(2)}) async-start(), calls=%async_computation.8 | async-start | bytes 1048576 | tf_op jit(solution)/shard_map/psum | solution.py:115
  54.3 19.6 %copy-start.3 = (f32[1024,128]{1,0:T(8,128)S(1)}, f32[1024,128]{1,0:T(8,128)}, u32[]{:S(2)}) copy-start(f32[1024,128]{1,0:T(8,128)} %custom-call) | copy-start | bytes 1572868
  112.2 12.3 %copy-start.6 = (bf16[1024,128]{1,0:T(8,128)(2,1)S(1)}, bf16[1024,128]{1,0:T(8,128)(2,1)}, u32[]{:S(2)}) copy-start(bf16[1024,128]{1,0:T(8,128)(2,1)} %get-tuple-element.283) | copy-start | bytes 786436 | tf_op jit(solution)/shard_map/while
  112.2 12.3 %copy-start.12 = (f32[128]{0:T(128)S(1)}, f32[128]{0:T(128)}, u32[]{:S(2)}) copy-start(f32[128]{0:T(128)} %get-tuple-element.284) | copy-start | bytes 1540 | tf_op jit(solution)/shard_map/while
  165.1 8.4 copy-start.1
  194.5 12.3 %copy-start.6 = (bf16[1024,128]{1,0:T(8,128)(2,1)S(1)}, bf16[1024,128]{1,0:T(8,128)(2,1)}, u32[]{:S(2)}) copy-start(bf16[1024,128]{1,0:T(8,128)(2,1)} %get-tuple-element.283) | copy-start | bytes 786436 | tf_op jit(solution)/shard_map/while
  194.5 12.3 %copy-start.12 = (f32[128]{0:T(128)S(1)}, f32[128]{0:T(128)}, u32[]{:S(2)}) copy-start(f32[128]{0:T(128)} %get-tuple-element.284) | copy-start | bytes 1540 | tf_op jit(solution)/shard_map/while
  247.4 8.4 copy-start.1
  276.8 12.3 %copy-start.6 = (bf16[1024,128]{1,0:T(8,128)(2,1)S(1)}, bf16[1024,128]{1,0:T(8,128)(2,1)}, u32[]{:S(2)}) copy-start(bf16[1024,128]{1,0:T(8,128)(2,1)} %get-tuple-element.283) | copy-start | bytes 786436 | tf_op jit(solution)/shard_map/while
  276.8 12.3 %copy-start.12 = (f32[128]{0:T(128)S(1)}, f32[128]{0:T(128)}, u32[]{:S(2)}) copy-start(f32[128]{0:T(128)} %get-tuple-element.284) | copy-start | bytes 1540 | tf_op jit(solution)/shard_map/while
  359.1 12.3 %copy-start.6 = (bf16[1024,128]{1,0:T(8,128)(2,1)S(1)}, bf16[1024,128]{1,0:T(8,128)(2,1)}, u32[]{:S(2)}) copy-start(bf16[1024,128]{1,0:T(8,128)(2,1)} %get-tuple-element.283) | copy-start | bytes 786436 | tf_op jit(solution)/shard_map/while
  359.1 12.3 %copy-start.12 = (f32[128]{0:T(128)S(1)}, f32[128]{0:T(128)}, u32[]{:S(2)}) copy-start(f32[128]{0:T(128)} %get-tuple-element.284) | copy-start | bytes 1540 | tf_op jit(solution)/shard_map/while
  441.4 12.3 %copy-start.6 = (bf16[1024,128]{1,0:T(8,128)(2,1)S(1)}, bf16[1024,128]{1,0:T(8,128)(2,1)}, u32[]{:S(2)}) copy-start(bf16[1024,128]{1,0:T(8,128)(2,1)} %get-tuple-element.283) | copy-start | bytes 786436 | tf_op jit(solution)/shard_map/while
  441.5 12.3 %copy-start.12 = (f32[128]{0:T(128)S(1)}, f32[128]{0:T(128)}, u32[]{:S(2)}) copy-start(f32[128]{0:T(128)} %get-tuple-element.284) | copy-start | bytes 1540 | tf_op jit(solution)/shard_map/while
  523.8 12.3 %copy-start.6 = (bf16[1024,128]{1,0:T(8,128)(2,1)S(1)}, bf16[1024,128]{1,0:T(8,128)(2,1)}, u32[]{:S(2)}) copy-start(bf16[1024,128]{1,0:T(8,128)(2,1)} %get-tuple-element.283) | copy-start | bytes 786436 | tf_op jit(solution)/shard_map/while
  523.8 12.3 %copy-start.12 = (f32[128]{0:T(128)S(1)}, f32[128]{0:T(128)}, u32[]{:S(2)}) copy-start(f32[128]{0:T(128)} %get-tuple-element.284) | copy-start | bytes 1540 | tf_op jit(solution)/shard_map/while
  606.1 12.3 %copy-start.6 = (bf16[1024,128]{1,0:T(8,128)(2,1)S(1)}, bf16[1024,128]{1,0:T(8,128)(2,1)}, u32[]{:S(2)}) copy-start(bf16[1024,128]{1,0:T(8,128)(2,1)} %get-tuple-element.283) | copy-start | bytes 786436 | tf_op jit(solution)/shard_map/while
  606.1 12.3 %copy-start.12 = (f32[128]{0:T(128)S(1)}, f32[128]{0:T(128)}, u32[]{:S(2)}) copy-start(f32[128]{0:T(128)} %get-tuple-element.284) | copy-start | bytes 1540 | tf_op jit(solution)/shard_map/while
  688.4 12.3 %copy-start.6 = (bf16[1024,128]{1,0:T(8,128)(2,1)S(1)}, bf16[1024,128]{1,0:T(8,128)(2,1)}, u32[]{:S(2)}) copy-start(bf16[1024,128]{1,0:T(8,128)(2,1)} %get-tuple-element.283) | copy-start | bytes 786436 | tf_op jit(solution)/shard_map/while
  688.4 12.3 %copy-start.12 = (f32[128]{0:T(128)S(1)}, f32[128]{0:T(128)}, u32[]{:S(2)}) copy-start(f32[128]{0:T(128)} %get-tuple-element.284) | copy-start | bytes 1540 | tf_op jit(solution)/shard_map/while
  752.9 99.1 %copy-start.2 = (bf16[1,1024,64]{1,2,0:T(8,128)(2,1)S(1)}, bf16[1,1024,64]{1,2,0:T(8,128)(2,1)}, u32[]{:S(2)}) copy-start(bf16[1,1024,64]{1,2,0:T(8,128)(2,1)} %param.7) | copy-start | bytes 393220
  752.9 99.1 %copy-start.8 = (f32[1024]{0:T(1024)S(1)}, f32[1024]{0:T(1024)}, u32[]{:S(2)}) copy-start(f32[1024]{0:T(1024)} %copy-done.7) | copy-start | bytes 12292
  752.9 99.1 %copy-start.10 = (f32[1024]{0:T(1024)S(1)}, f32[1024]{0:T(1024)}, u32[]{:S(2)}) copy-start(f32[1024]{0:T(1024)} %copy-done.9) | copy-start | bytes 12292
  757.9 10.3 %all-to-all-start.2 = ((bf16[32,128,32]{1,2,0:T(8,128)(2,1)}), bf16[32,128,32]{1,2,0:T(8,128)(2,1)S(1)}, u32[]{:S(2)}, u32[]{:S(2)}) async-start(bf16[32,128,32]{1,2,0:T(8,128)(2,1)} %copy.67), calls=%async_computation.2 | async-start | bytes 524288 | tf_op jit(solution)/shard_map/all_to_all | solution.py:101
  768.2 25.7 %all-to-all-start.3 = ((bf16[32,256,32]{1,2,0:T(8,128)(2,1)}), bf16[32,256,32]{1,2,0:T(8,128)(2,1)S(1)}, u32[]{:S(2)}, u32[]{:S(2)}) async-start(bf16[32,256,32]{1,2,0:T(8,128)(2,1)} %bitcast.20), calls=%async_computation.4 | async-start | bytes 1048576 | tf_op jit(solution)/shard_map/all_to_all | solution.py:107
  771.6 44.3 %reduce-scatter.3.cloned.1.call-start = ((), (), s32[]{:S(2)}) async-start(), calls=%async_computation.6 | async-start | bytes 327680 | tf_op jit(solution)/shard_map/reduce_scatter | solution.py:104
  772.5 79.5 %reduce-scatter.5.cloned.1.call-start = ((), (), s32[]{:S(2)}) async-start(), calls=%async_computation.7 | async-start | bytes 589824 | tf_op jit(solution)/shard_map/reduce_scatter | solution.py:114
  794.8 115.0 %all-reduce.5.cloned.1.call-start = ((), (), s32[]{:S(2)}) async-start(), calls=%async_computation.9 | async-start | bytes 1048576 | tf_op jit(solution)/shard_map/psum | solution.py:115
  (10 other events, 56.5 us)
Sparse Core Ops, SparseCore 0:
  753.8 40.7 all-reduce.2
  796.9 18.9 reduce-scatter.2
  819.6 32.3 reduce-scatter.4
  855.0 54.7 all-reduce.4
